TPU v7x, 128 devices: a whole 4x4x4 slice. The times are simulated.
128 devices in a mesh: req: 32 (over x, z, core), tp: 4 (over y).
Axes of the slice: x: 4, y: 4, z: 4, core: 2. Of those that a mesh axis runs over, the one named last changes fastest.
Arguments:
- tokens: bfloat16 [65536, 1024], P('req'), may hold values from -6 to 6
- attn_gain: bfloat16 [1024], replicated, may hold values from 0.5 to 1.5
- w_query: bfloat16 [1024, 1024], P(None, 'tp'), may hold values from -1 to 1
- w_key: bfloat16 [1024, 1024], P(None, 'tp'), may hold values from -1 to 1
- w_value: bfloat16 [1024, 1024], P(None, 'tp'), may hold values from -0.1875 to 0.1875
- persist_key: bfloat16 [16, 1024], P(None, 'tp'), may hold values from -250 to 250
- persist_value: bfloat16 [16, 1024], P(None, 'tp'), may hold values from -6 to 6
- log_forget: float32 [65536, 8], P('req', 'tp'), may hold values from -0.75 to 0
- mem_gain: float32 [1024], P('tp'), may hold values from 0.5 to 1.5
- w_out: bfloat16 [1024, 1024], P('tp'), may hold values from -0.1875 to 0.1875
- ffn_gain: bfloat16 [1024], replicated, may hold values from 0.5 to 1.5
- w_gate: bfloat16 [1024, 2816], P(None, 'tp'), may hold values from -0.1875 to 0.1875
- w_up: bfloat16 [1024, 2816], P(None, 'tp'), may hold values from -0.1875 to 0.1875
- w_down: bfloat16 [2816, 1024], P('tp'), may hold values from -0.109375 to 0.109375
- doc_ids: int32 [65536], P('req'), may hold values from 0 to 512, never falling along the last dimension, each value on 1 to 32768 neighbouring positions
- page_owner: int32 [512], P('req'), may hold values from 0 to 31, as said below
- page_slot: int32 [512], P('req'), may hold values from 0 to 15
Outputs:
- layer_out: bfloat16 [65536, 1024], P('req')
- kv_cache: bfloat16 [512, 128, 2048], P('req', None, 'tp')
Inputs may be any that keep to these rules, and one draw needn't show every extreme that they name: `page_owner`: the pages of one index of req going to one owner number at most 1, and every owner receives exactly 16 pages, one for each of its slots.
All inputs are finite; a program needn't handle non-finite values.
Results may differ from a plain program's by a relative error of at most 0.015.
Values may be sent and summed in bfloat16 or wider, within the bound.
No kernel may reach another device: no remote copies, remote signals or barrier semaphores. Data moves between devices by JAX's collectives and lax.ppermute only.
A program may use at most 128 MiB of HBM per device.

v0:
```python
import math
import jax
import jax.numpy as jnp
from jax import lax
from jax.sharding import PartitionSpec as P

HEAD_DIM = 128
PERSIST = 16
SEG = 1024
PAGE = 128
norm_eps = 1e-05
unit_eps = 1e-06
big_negative = -1e30


def entering(shard, axis, combine, identity):
    devices, position = (lax.axis_size(axis), lax.axis_index(axis))
    everything = jax.tree.map(lambda part: lax.all_gather(part, axis), shard)
    start = jax.tree.map(
        lambda part, zero: jnp.broadcast_to(jnp.asarray(zero, part.dtype), part.shape),
        shard,
        identity,
    )

    def step(k, before):
        reached = k < position
        new = combine(before, jax.tree.map(lambda part: part[k], everything))
        return jax.tree.map(lambda a, b: jnp.where(reached, a, b), new, before)

    return lax.fori_loop(0, devices, step, start)


def rms_scale(values, gain):
    wide = values.astype(jnp.float32)
    return (
        wide
        * lax.rsqrt(jnp.mean(wide * wide, axis=-1, keepdims=True) + norm_eps)
        * gain.astype(jnp.float32)
    )


def unit_rows(values):
    wide = values.astype(jnp.float32)
    return (
        wide
        * lax.rsqrt(jnp.mean(wide * wide, axis=-1, keepdims=True) + unit_eps)
        / math.sqrt(wide.shape[-1])
    )


def attend(queries, key_rows, value_rows, docs, persist_keys, persist_values):
    scale = 1.0 / math.sqrt(queries.shape[-1])
    local = (
        jnp.einsum("thd,shd->hts", queries, key_rows, preferred_element_type=jnp.float32) * scale
    )
    order = jnp.arange(docs.shape[0])
    allowed = (order[None, :] <= order[:, None]) & (docs[None, :] == docs[:, None])
    local = jnp.where(allowed[None], local, big_negative)
    persist = (
        jnp.einsum("thd,phd->htp", queries, persist_keys, preferred_element_type=jnp.float32)
        * scale
    )
    peak = jnp.maximum(jnp.max(persist, axis=-1), jnp.max(local, axis=-1))
    weight_persist = jnp.exp(persist - peak[..., None])
    weight_local = jnp.exp(local - peak[..., None])
    total = jnp.sum(weight_persist, axis=-1) + jnp.sum(weight_local, axis=-1)
    probs_persist = (weight_persist / total[..., None]).astype(jnp.bfloat16)
    probs_local = (weight_local / total[..., None]).astype(jnp.bfloat16)
    return jnp.einsum(
        "htp,phd->thd", probs_persist, persist_values, preferred_element_type=jnp.float32
    ) + jnp.einsum("hts,shd->thd", probs_local, value_rows, preferred_element_type=jnp.float32)


def memory_block(carry, inputs):
    state, carried = carry
    q_unit, k_unit, value_rows, decay_log, docs = inputs
    value_wide = value_rows.astype(jnp.float32)
    cumul = jnp.cumsum(decay_log, axis=0)
    diff = cumul[:, None, :] - cumul[None, :, :]
    order = jnp.arange(docs.shape[0])
    allowed = ((order[None, :] <= order[:, None]) & (docs[None, :] == docs[:, None]))[:, :, None]
    decay = jnp.where(allowed, jnp.exp(jnp.where(allowed, diff, 0.0)), 0.0)
    inner = jnp.einsum("thd,shd->tsh", q_unit, k_unit, precision=lax.Precision.HIGHEST) * decay
    recall = jnp.einsum("tsh,shd->thd", inner, value_wide, precision=lax.Precision.HIGHEST)
    continues = (docs == carried).astype(jnp.float32)
    reach = jnp.exp(cumul) * continues[:, None]
    recall = (
        recall
        + jnp.einsum("thd,hde->the", q_unit, state, precision=lax.Precision.HIGHEST)
        * reach[:, :, None]
    )
    last_doc = docs[-1]
    keep = jnp.exp(cumul[-1][None, :] - cumul) * (docs == last_doc).astype(jnp.float32)[:, None]
    kept = jnp.exp(cumul[-1]) * (last_doc == carried).astype(jnp.float32)
    state_next = (
        jnp.einsum(
            "shd,she->hde", k_unit * keep[:, :, None], value_wide, precision=lax.Precision.HIGHEST
        )
        + state * kept[:, None, None]
    )
    return ((state_next, last_doc), recall)


def combine_maps(earlier, later):
    joins = jnp.logical_or(
        jnp.logical_or(earlier[3] == later[2], earlier[3] < 0), later[2] < 0
    ).astype(jnp.float32)
    carry_factor = later[0] * joins
    return (
        carry_factor * earlier[0],
        carry_factor[:, None, None] * earlier[1] + later[1],
        jnp.where(earlier[2] < 0, later[2], earlier[2]),
        jnp.where(later[3] < 0, earlier[3], later[3]),
    )


def place_pages(key3, value3, page_owner, page_slot):
    page_count = page_owner.shape[0]
    req_count = lax.axis_size("req")
    capacity = max(1, page_count // req_count)
    pages = jnp.stack([key3, value3], axis=2).reshape(page_count, -1)
    order = jnp.arange(page_count)
    same_owner = page_owner[:, None] == page_owner[None, :]
    rank = jnp.sum((same_owner & (order[:, None] < order[None, :])).astype(jnp.int32), axis=0)
    bucket = page_owner * capacity + rank
    targets = jnp.arange(req_count * capacity)
    routing = targets[:, None] == bucket[None, :]
    outgoing = jnp.dot(
        routing.astype(jnp.bfloat16), pages, preferred_element_type=jnp.float32
    ).astype(jnp.bfloat16)
    outgoing = outgoing.reshape(req_count, capacity, -1)
    codes = (jnp.sum(routing.astype(jnp.int32) * (page_slot[None, :] + 1), axis=1) - 1).astype(
        jnp.bfloat16
    )
    codes = codes.reshape(req_count, capacity)
    arrived, arrived_codes = (
        lax.all_to_all(outgoing, "req", split_axis=0, concat_axis=0, tiled=True),
        lax.all_to_all(codes, "req", split_axis=0, concat_axis=0, tiled=True),
    )
    wanted = (
        arrived_codes.reshape(-1).astype(jnp.float32)[None, :]
        == jnp.arange(page_count).astype(jnp.float32)[:, None]
    )
    cache = jnp.dot(
        wanted.astype(jnp.bfloat16),
        arrived.reshape(req_count * capacity, -1),
        preferred_element_type=jnp.float32,
    )
    return cache.astype(jnp.bfloat16).reshape(page_count, PAGE, -1)


def on_device(
    tokens,
    attn_gain,
    w_query,
    w_key,
    w_value,
    persist_key,
    persist_value,
    log_forget,
    mem_gain,
    w_out,
    ffn_gain,
    w_gate,
    w_up,
    w_down,
    doc_ids,
    page_owner,
    page_slot,
):
    tok_count = tokens.shape[0]
    heads_here = w_query.shape[1] // HEAD_DIM
    normed = rms_scale(tokens, attn_gain).astype(jnp.bfloat16)
    queries = jnp.dot(normed, w_query, preferred_element_type=jnp.float32).astype(jnp.bfloat16)
    key_rows = jnp.dot(normed, w_key, preferred_element_type=jnp.float32).astype(jnp.bfloat16)
    value_rows = jnp.dot(normed, w_value, preferred_element_type=jnp.float32).astype(jnp.bfloat16)
    shape3 = (tok_count, heads_here, HEAD_DIM)
    kv_cache = place_pages(
        key_rows.reshape(shape3), value_rows.reshape(shape3), page_owner, page_slot
    )
    blocks = tok_count // SEG
    shape4 = (blocks, SEG, heads_here, HEAD_DIM)
    q_unit = unit_rows(queries.reshape(shape3))
    k_unit = unit_rows(key_rows.reshape(shape3))
    doc_blocks = doc_ids.reshape(blocks, SEG)
    mem_rows = math.gcd(tok_count, 512)
    mem_blocks = tok_count // mem_rows
    mem_shape = (mem_blocks, mem_rows, heads_here, HEAD_DIM)
    start = (jnp.zeros((heads_here, HEAD_DIM, HEAD_DIM), jnp.float32), jnp.int32(-1))
    finish, recall = lax.scan(
        memory_block,
        start,
        (
            q_unit.reshape(mem_shape),
            k_unit.reshape(mem_shape),
            value_rows.reshape(mem_shape),
            log_forget.reshape(mem_blocks, mem_rows, heads_here),
            doc_ids.reshape(mem_blocks, mem_rows),
        ),
    )
    local_state = finish[0]
    recall = recall.reshape(shape3)
    cumul = jnp.cumsum(log_forget, axis=0)
    whole_doc = (doc_ids[0] == doc_ids[-1]).astype(jnp.float32)
    element = (
        jnp.exp(cumul[-1]) * whole_doc,
        local_state,
        doc_ids[0].astype(jnp.float32),
        doc_ids[-1].astype(jnp.float32),
    )
    identity = (
        jnp.ones((heads_here,), jnp.float32),
        jnp.zeros_like(local_state),
        jnp.float32(-1.0),
        jnp.float32(-1.0),
    )
    prefix = entering(element, "req", combine_maps, identity)
    continues = (doc_ids.astype(jnp.float32) == prefix[3]).astype(jnp.float32)
    reach = jnp.exp(cumul) * continues[:, None]
    recall = (
        recall
        + jnp.einsum("thd,hde->the", q_unit, prefix[1], precision=lax.Precision.HIGHEST)
        * reach[:, :, None]
    )
    persist_keys = persist_key.reshape(PERSIST, heads_here, HEAD_DIM)
    persist_values = persist_value.reshape(PERSIST, heads_here, HEAD_DIM)

    def attend_block(parts):
        return attend(parts[0], parts[1], parts[2], parts[3], persist_keys, persist_values)

    attended = lax.map(
        attend_block,
        (queries.reshape(shape4), key_rows.reshape(shape4), value_rows.reshape(shape4), doc_blocks),
    )
    memory_out = rms_scale(recall, mem_gain.reshape(heads_here, HEAD_DIM))
    heads_out = (
        (attended.reshape(shape3) + memory_out)
        .astype(jnp.bfloat16)
        .reshape(tok_count, heads_here * HEAD_DIM)
    )
    head_total = lax.psum(jnp.dot(heads_out, w_out, preferred_element_type=jnp.float32), "tp")
    resid = (tokens.astype(jnp.float32) + head_total).astype(jnp.bfloat16)
    normed_ffn = rms_scale(resid, ffn_gain).astype(jnp.bfloat16)
    gate_proj = jnp.dot(normed_ffn, w_gate, preferred_element_type=jnp.float32)
    up_proj = jnp.dot(normed_ffn, w_up, preferred_element_type=jnp.float32)
    hidden = (jax.nn.silu(gate_proj) * up_proj).astype(jnp.bfloat16)
    unit_total = lax.psum(
        jnp.dot(hidden, w_down, preferred_element_type=jnp.float32).astype(jnp.bfloat16), "tp"
    ).astype(jnp.float32)
    layer_out = (resid.astype(jnp.float32) + unit_total).astype(jnp.bfloat16)
    return (layer_out, kv_cache)


def solution(mesh):
    return jax.shard_map(
        on_device,
        mesh=mesh,
        in_specs=(
            P("req", None),
            P(),
            P(None, "tp"),
            P(None, "tp"),
            P(None, "tp"),
            P(None, "tp"),
            P(None, "tp"),
            P("req", "tp"),
            P("tp"),
            P("tp", None),
            P(),
            P(None, "tp"),
            P(None, "tp"),
            P("tp", None),
            P("req"),
            P("req"),
            P("req"),
        ),
        out_specs=(P("req", None), P("req", None, "tp")),
        check_vma=False,
    )
```

profile of v0, /device:TPU:1, one launch (start us, length us, event | category | flops | bytes accessed | tf_op | source)
XLA Modules:
  0.0 916.4 jit_solution(10726321676844413340)
XLA Ops:
  40.2 113.1 %while.42 = (s32[]{:T(128)}, f32[2,128,128]{2,1,0:T(8,128)}, s32[]{:T(128)}, f32[4,512,2,128]{1,0,3,2:T(4,128)}, f32[4,512,2,128]{3,1,2,0:T(8,128)}, /*index=5*/...) while((s32[]{:T(128)}, f32[2,128,128]{2,1,0:T(8,128)}, ...), condition=%wide.region_12.13_spmd.clone, body=%wide.region_9.12_spmd.clone.sunk | while | flops 2016809984 | bytes 11492285 | solution.py:190
  56.8 11.1 %dynamic_update_slice.12 = f32[4,512,2,128]{1,0,3,2:T(4,128)} dynamic-update-slice(f32[4,512,2,128]{1,0,3,2:T(4,128)} %get-tuple-element.758, f32[1,512,2,128]{1,0,3,2:T(1,128)S(1)} %copy.278, s32[]{:T(128)S(6)} %copy.291, s32[]{:T(128)} %constant.104.clone.1..sunk.1, s32[]{:T(128)} %constant.104.clone.1..sunk.1, s32[]{:T(128)} %constant.104.clone.1..sunk.1) | dynamic-update-slice | bytes 1048580 | tf_op jit(solution)/shard_map/while/body/jit(dynamic_update_index_in_dim)/dynamic_update_slice | solution.py:190
  85.1 11.1 %dynamic_update_slice.12 = f32[4,512,2,128]{1,0,3,2:T(4,128)} dynamic-update-slice(f32[4,512,2,128]{1,0,3,2:T(4,128)} %get-tuple-element.758, f32[1,512,2,128]{1,0,3,2:T(1,128)S(1)} %copy.278, s32[]{:T(128)S(6)} %copy.291, s32[]{:T(128)} %constant.104.clone.1..sunk.1, s32[]{:T(128)} %constant.104.clone.1..sunk.1, s32[]{:T(128)} %constant.104.clone.1..sunk.1) | dynamic-update-slice | bytes 1048580 | tf_op jit(solution)/shard_map/while/body/jit(dynamic_update_index_in_dim)/dynamic_update_slice | solution.py:190
  113.4 11.1 %dynamic_update_slice.12 = f32[4,512,2,128]{1,0,3,2:T(4,128)} dynamic-update-slice(f32[4,512,2,128]{1,0,3,2:T(4,128)} %get-tuple-element.758, f32[1,512,2,128]{1,0,3,2:T(1,128)S(1)} %copy.278, s32[]{:T(128)S(6)} %copy.291, s32[]{:T(128)} %constant.104.clone.1..sunk.1, s32[]{:T(128)} %constant.104.clone.1..sunk.1, s32[]{:T(128)} %constant.104.clone.1..sunk.1) | dynamic-update-slice | bytes 1048580 | tf_op jit(solution)/shard_map/while/body/jit(dynamic_update_index_in_dim)/dynamic_update_slice | solution.py:190
  141.6 11.1 %dynamic_update_slice.12 = f32[4,512,2,128]{1,0,3,2:T(4,128)} dynamic-update-slice(f32[4,512,2,128]{1,0,3,2:T(4,128)} %get-tuple-element.758, f32[1,512,2,128]{1,0,3,2:T(1,128)S(1)} %copy.278, s32[]{:T(128)S(6)} %copy.291, s32[]{:T(128)} %constant.104.clone.1..sunk.1, s32[]{:T(128)} %constant.104.clone.1..sunk.1, s32[]{:T(128)} %constant.104.clone.1..sunk.1) | dynamic-update-slice | bytes 1048580 | tf_op jit(solution)/shard_map/while/body/jit(dynamic_update_index_in_dim)/dynamic_update_slice | solution.py:190
  172.1 64.1 %while.41 = (s32[]{:T(128)}, f32[2,1024,2,128]{1,0,3,2:T(2,128)}, bf16[2,1024,2,128]{3,1,2,0:T(8,128)(2,1)}, bf16[16,2,128]{2,0,1:T(8,128)(2,1)S(1)}, s32[2,1024...) while((s32[]{:T(128)}, f32[2,1024,2,128]{1,0,3,2:T(2,128)}, ...), condition=%wide.region_6.7_spmd, body=%wide.region_1.6_spmd.sunk | while | flops 1119318016 | bytes 39351420 | solution.py:231
  185.4 18.9 %dynamic_update_slice.11 = f32[2,1024,2,128]{1,0,3,2:T(2,128)} dynamic-update-slice(f32[2,1024,2,128]{1,0,3,2:T(2,128)} %get-tuple-element.723, f32[1,1024,2,128]{1,0,3,2:T(1,128)S(1)} %copy.275, s32[]{:T(128)S(6)} %copy.283, s32[]{:T(128)} %constant.104.clone.1..sunk, s32[]{:T(128)} %constant.104.clone.1..sunk, s32[]{:T(128)} %constant.104.clone.1..sunk) | dynamic-update-slice | bytes 2097156 | tf_op jit(solution)/shard_map/while/body/jit(dynamic_update_index_in_dim)/dynamic_update_slice | solution.py:231
  217.5 18.8 %dynamic_update_slice.11 = f32[2,1024,2,128]{1,0,3,2:T(2,128)} dynamic-update-slice(f32[2,1024,2,128]{1,0,3,2:T(2,128)} %get-tuple-element.723, f32[1,1024,2,128]{1,0,3,2:T(1,128)S(1)} %copy.275, s32[]{:T(128)S(6)} %copy.283, s32[]{:T(128)} %constant.104.clone.1..sunk, s32[]{:T(128)} %constant.104.clone.1..sunk, s32[]{:T(128)} %constant.104.clone.1..sunk) | dynamic-update-slice | bytes 2097156 | tf_op jit(solution)/shard_map/while/body/jit(dynamic_update_index_in_dim)/dynamic_update_slice | solution.py:231
  258.4 26.0 %all-gather.1 = f32[32,1,2]{2,1,0:T(1,128)} all-gather(f32[1,1,2]{2,1,0:T(1,128)S(1)} %bitcast.265), channel_id=1, replica_groups=mesh['req'=32,'tp'=4] {'req'}, dimensions={0}, use_global_device_ids=true | all-gather | bytes 264 | tf_op jit(solution)/shard_map/all_gather | solution.py:18
  289.4 62.7 %all-reduce.2 = (f32[32]{0:T(128)}, f32[32]{0:T(128)}) all-reduce(f32[32]{0:T(128)} %convert_dynamic-update-slice_fusion.1, f32[32]{0:T(128)} %convert_dynamic-update-slice_fusion), channel_id=1, replica_groups=mesh['req'=32,'tp'=4] {'req'}, use_global_device_ids=true, to_apply=%add | all-reduce | flops 64 | bytes 512
  352.1 255.1 %while.43 = (s32[]{:T(128)}, f32[2,128,128]{2,1,0:T(8,128)}, f32[]{:T(128)}, s32[]{:T(128)}, f32[32,2]{1,0:T(8,128)}, /*index=5*/f32[32]{0:T(128)}, f32[32,2,128...) while((s32[]{:T(128)}, f32[2,128,128]{2,1,0:T(8,128)}, ...), condition=%wide.region_16.17_spmd.clone, body=%wide.region_15.16_spmd.clone.sunk | while | flops 131087 | bytes 393486 | solution.py:30
  620.8 6.2 all-to-all-start
  635.8 5.7 pad_maximum_fusion
  649.6 6.8 reduce.10
  656.4 6.6 reshape.365
  663.0 114.6 %all-reduce.6.cloned.1.call-done = f32[2048,1024]{1,0:T(8,128)} async-done(((f32[2048,1024]{1,0:T(8,128)}), f32[2048,1024]{1,0:T(8,128)}) %all-reduce.6.cloned.1.call-update) | async-done | bytes 8388624 | tf_op jit(solution)/shard_map/psum | solution.py:241
  777.6 5.9 fusion.66
  790.6 7.9 all-to-all-start.1
  798.7 10.8 %convolution_convert_fusion.2 = bf16[2048,1024]{1,0:T(8,128)(2,1)} fusion(bf16[704,1024]{1,0:T(8,128)(2,1)S(1)} %copy-done, f32[2048,704]{0,1:T(8,128)} %fusion.78, bf16[1024,704]{0,1:T(8,128)(2,1)S(1)} %copy-done.24, bf16[2048,1024]{1,0:T(8,128)(2,1)} %copy-done.1, f32[1024]{0:T(1024)S(1)} %copy-done.20, f32[2048]{0:T(1024)S(1)} %add_rsqrt_fusion.3), kind=kOutput, calls=%fused_computation.108 | convolution fusion | flops 5924716544 | bytes 17051648 | tf_op jit(solution)/shard_map/dot_general | solution.py:248
  809.9 40.8 %all-to-all-done.1 = bf16[32,2,32768]{2,1,0:T(2,128)(2,1)} async-done(((bf16[32,2,32768]{2,1,0:T(2,128)(2,1)}), bf16[32,2,32768]{2,1,0:T(2,128)(2,1)}, u32[]{:S(2)}, u32[]{:S(2)}) %all-to-all-start.1) | async-done | bytes 4194336 | tf_op jit(solution)/shard_map/all_to_all | solution.py:137
  850.7 19.8 %reshape.366 = bf16[32,1,65536]{2,1,0:T(2,128)(2,1)} reshape(bf16[32,2,32768]{2,1,0:T(2,128)(2,1)} %all-to-all-done.1) | data formatting | bytes 8388608
  870.6 8.0 convolution_convert_fusion.1
  880.6 21.5 %all-reduce.8.cloned.1.call-done = bf16[2048,1024]{1,0:T(8,128)(2,1)} async-done(((bf16[2048,1024]{1,0:T(8,128)(2,1)}), bf16[2048,1024]{1,0:T(8,128)(2,1)}) %all-reduce.8.cloned.1.call-update) | async-done | bytes 4194320 | tf_op jit(solution)/shard_map/psum | solution.py:247
  902.1 7.6 fusion.69
  (360 shorter events, 381.4 us)
Async XLA Ops:
  7.2 791.6 %copy-start = (bf16[704,1024]{1,0:T(8,128)(2,1)S(1)}, bf16[704,1024]{1,0:T(8,128)(2,1)}, u32[]{:S(2)}) copy-start(bf16[704,1024]{1,0:T(8,128)(2,1)} %param.36) | copy-start | bytes 4325380
  7.2 344.9 %all-gather.4.cloned.1.call-start = ((), (), s32[]{:S(2)}) async-start(), calls=%async_computation.4 | async-start | bytes 4325376 | tf_op jit(solution)/shard_map/all_gather | solution.py:18
  7.2 4.2 copy-start.2
  15.1 5.1 copy-start.5
  17.6 9.0 copy-start.3
  25.7 7.7 copy-start.7
  26.6 9.4 %copy-start.13 = (f32[2048,2]{0,1:T(2,128)}, f32[2048,2]{0,1:T(2,128)S(1)}, u32[]{:S(2)}) copy-start(f32[2048,2]{0,1:T(2,128)S(1)} %add_rsqrt_fusion.1) | copy-start | bytes 49156
  153.3 7.0 copy-start.8
  153.3 8.6 copy-start.6
  153.3 624.3 %all-reduce.6.cloned.1.call-start = ((), (), s32[]{:S(2)}) async-start(), calls=%async_computation.2 | async-start | bytes 16777216 | tf_op jit(solution)/shard_map/psum | solution.py:241
  161.9 9.0 copy-start.11
  163.5 8.7 copy-start.18
  163.5 8.7 copy-start.19
  243.0 365.9 %copy-start.14 = (f32[2048,2]{0,1:T(2,128)S(1)}, f32[2048,2]{0,1:T(2,128)}, u32[]{:S(2)}) copy-start(f32[2048,2]{0,1:T(2,128)} %copy-done.13) | copy-start | bytes 49156
  607.2 6.0 copy-start.10
  607.2 6.0 copy-start.21
  618.7 9.6 %copy-start.9 = (bf16[2048,256]{0,1:T(8,128)(2,1)S(1)}, bf16[2048,256]{0,1:T(8,128)(2,1)}, u32[]{:S(2)}) copy-start(bf16[2048,256]{0,1:T(8,128)(2,1)} %convolution_convert_fusion.3) | copy-start | bytes 3145732
  618.7 13.3 %copy-start.4 = (bf16[2048,256]{0,1:T(8,128)(2,1)S(1)}, bf16[2048,256]{0,1:T(8,128)(2,1)}, u32[]{:S(2)}) copy-start(bf16[2048,256]{0,1:T(8,128)(2,1)} %copy-done.3) | copy-start | bytes 3145732
  620.8 169.8 %all-to-all-start = ((bf16[32,1,1]{2,1,0:T(2,128)(2,1)}), bf16[32,1,1]{2,1,0:T(2,128)(2,1)S(1)}, u32[]{:S(2)}, u32[]{:S(2)}) async-start(bf16[32,1,1]{2,1,0:T(2,128)(2,1)} %copy.222), calls=%async_computation | async-start | bytes 32768 | tf_op jit(solution)/shard_map/all_to_all | solution.py:138
  663.0 122.5 %copy-start.20 = (f32[1024]{0:T(1024)S(1)}, f32[1024]{0:T(1024)}, u32[]{:S(2)}) copy-start(f32[1024]{0:T(1024)} %convert_element_type.185) | copy-start | bytes 12292
  663.0 122.5 %copy-start.23 = (bf16[1024,704]{0,1:T(8,128)(2,1)S(1)}, bf16[1024,704]{0,1:T(8,128)(2,1)}, u32[]{:S(2)}) copy-start(bf16[1024,704]{0,1:T(8,128)(2,1)} %param.34) | copy-start | bytes 4325380
  790.6 8.1 copy-start.24
  790.6 60.1 %all-to-all-start.1 = ((bf16[32,2,32768]{2,1,0:T(2,128)(2,1)}), bf16[32,2,32768]{2,1,0:T(2,128)(2,1)}, u32[]{:S(2)}, u32[]{:S(2)}) async-start(bf16[32,2,32768]{2,1,0:T(2,128)(2,1)} %reshape.365), calls=%async_computation.1 | async-start | bytes 8388608 | tf_op jit(solution)/shard_map/all_to_all | solution.py:137
  798.5 103.6 %all-reduce.8.cloned.1.call-start = ((), (), s32[]{:S(2)}) async-start(), calls=%async_computation.3 | async-start | bytes 8388608 | tf_op jit(solution)/shard_map/psum | solution.py:247
  (10 other events, 18.3 us)
Sparse Core Ops, SparseCore 0:
  153.5 49.9 all-gather.3
  618.9 158.6 all-reduce.5
  809.7 92.3 all-reduce.7
where the time goes:
time: 932 us; the launch traced here: 916 us
  local copies, waits for them, and re-layouts  271 us (29%)
  waiting for transfers between devices  177 us (19%)
  other arithmetic  156 us (17%)
  matrix products  107 us (11%)
  blocking collectives  88.7 us (10%)
  loops' own time  86.5 us (9%)
  between operations  15.5 us (2%)
  starting transfers between devices  14.3 us (2%)
    psum x1, waiting for transfers between devices, on_device(): lax.psum(jnp.dot(heads_out, w_out, preferred_element_type=jnp.float32), '...  115 us
    another operation x1, loops' own time, entering(): return lax.fori_loop(0, devices, step, start)  81.6 us
    dynamic_slice x64, local copies, waits for them, and re-layouts, step(): new = combine(before, jax.tree.map(lambda part: part[k], everything))  79.4 us
    unnamed x1, blocking collectives  62.7 us
    select_n x32, other arithmetic, step(): return jax.tree.map(lambda a, b: jnp.where(reached, a, b), new, before)  54.3 us
    dynamic_update_slice x8, local copies, waits for them, and re-layouts, on_device(): lax.scan(memory_block, start, (q_unit.reshape(mem_shape), k_unit.reshape(...  46.6 us
    all_to_all x1, waiting for transfers between devices, place_pages(): lax.all_to_all(outgoing, 'req', split_axis=0, concat_axis=0, tiled=True)  40.8 us
    mul x32, other arithmetic, combine_maps(): carry_factor = later[0] * joins  39.9 us
  transfers between devices with their start and end apart: 5, of which 3 were waited for; matrix products, arithmetic and copies ran while one was open for 21% of the time, Pallas kernels for 0%

commit v1 on v0

--- a/solution.py
+++ b/solution.py
@@ -244,8 +244,11 @@
     gate_proj = jnp.dot(normed_ffn, w_gate, preferred_element_type=jnp.float32)
     up_proj = jnp.dot(normed_ffn, w_up, preferred_element_type=jnp.float32)
     hidden = (jax.nn.silu(gate_proj) * up_proj).astype(jnp.bfloat16)
-    unit_total = lax.psum(
-        jnp.dot(hidden, w_down, preferred_element_type=jnp.float32).astype(jnp.bfloat16), "tp"
+    unit_total = jnp.sum(
+        lax.all_gather(
+            jnp.dot(hidden, w_down, preferred_element_type=jnp.float32).astype(jnp.bfloat16), "tp"
+        ),
+        axis=0,
     ).astype(jnp.float32)
     layer_out = (resid.astype(jnp.float32) + unit_total).astype(jnp.bfloat16)
     return (layer_out, kv_cache)

time: 932 us -> 970 us (1.041)
  waiting for transfers between devices: 177 us -> 229 us
    psum x1, waiting for transfers between devices: 115 us -> 158 us  [on_device(): lax.psum(jnp.dot(heads_out, w_out, preferred_element_type=jnp.float32), '...]
    psum x1 -> x0, waiting for transfers between devices: 21.5 us -> none  [on_device(): lax.psum(jnp.dot(hidden, w_down, preferred_element_type=jnp.float32).asty...]
    all_gather x0 -> x1, waiting for transfers between devices: none -> 19.3 us  [on_device(): lax.all_gather(jnp.dot(hidden, w_down, preferred_element_type=jnp.float32...]
    mul x32, other arithmetic: 39.9 us -> 22.1 us  [combine_maps(): carry_factor = later[0] * joins]
    reduce_sum x0 -> x1, other arithmetic: none -> 12 us  [on_device(): jnp.sum(lax.all_gather(jnp.dot(hidden, w_down, preferred_element_type=jnp...]
    all_to_all x1, waiting for transfers between devices: 40.8 us -> 51.7 us  [place_pages(): lax.all_to_all(outgoing, 'req', split_axis=0, concat_axis=0, tiled=True)]
    unnamed x67 -> x59, local copies, waits for them, and re-layouts: 39 us -> 40.4 us
  transfers between devices with their start and end apart: 5 -> 5, of which waited for: 3 -> 3; matrix products, arithmetic and copies ran while one was open for 21% -> 18% of each run, Pallas kernels for 0% -> 0%
where the time goes in v1:
time: 970 us; the launch traced here: 954 us
  local copies, waits for them, and re-layouts  268 us (28%)
  waiting for transfers between devices  229 us (24%)
  other arithmetic  147 us (15%)
  matrix products  103 us (11%)
  blocking collectives  88.7 us (9%)
  loops' own time  85.9 us (9%)
  starting transfers between devices  16.2 us (2%)
  between operations  15.6 us (2%)
    psum x1, waiting for transfers between devices, on_device(): lax.psum(jnp.dot(heads_out, w_out, preferred_element_type=jnp.float32), '...  158 us
    dynamic_slice x64, local copies, waits for them, and re-layouts, step(): new = combine(before, jax.tree.map(lambda part: part[k], everything))  81.9 us
    another operation x1, loops' own time, entering(): return lax.fori_loop(0, devices, step, start)  80.2 us
    unnamed x1, blocking collectives  62.8 us
    select_n x32, other arithmetic, step(): return jax.tree.map(lambda a, b: jnp.where(reached, a, b), new, before)  54.2 us
    all_to_all x1, waiting for transfers between devices, place_pages(): lax.all_to_all(outgoing, 'req', split_axis=0, concat_axis=0, tiled=True)  51.7 us
    dynamic_update_slice x8, local copies, waits for them, and re-layouts, on_device(): lax.scan(memory_block, start, (q_unit.reshape(mem_shape), k_unit.reshape(...  46.5 us
    unnamed x59, local copies, waits for them, and re-layouts  40.4 us
  transfers between devices with their start and end apart: 5, of which 3 were waited for; matrix products, arithmetic and copies ran while one was open for 18% of the time, Pallas kernels for 0%

profile of v1, /device:TPU:1, one launch (start us, length us, event | category | flops | bytes accessed | tf_op | source)
XLA Modules:
  0.0 954.2 jit_solution(13572917156794966078)
XLA Ops:
  42.5 100.3 %while.42 = (s32[]{:T(128)}, f32[2,128,128]{2,1,0:T(8,128)S(1)}, s32[]{:T(128)}, f32[4,512,2,128]{1,0,3,2:T(4,128)}, f32[4,512,2,128]{3,1,2,0:T(8,128)}, /*index...) while((s32[]{:T(128)}, f32[2,128,128]{2,1,0:T(8,128)S(1)}, ...), condition=%wide.region_12.13_spmd.clone, body=%wide.region_9.12_spmd.clone.sunk | while | flops 2016809984 | bytes 11492285 | solution.py:190
  55.9 11.1 %dynamic_update_slice.12 = f32[4,512,2,128]{1,0,3,2:T(4,128)} dynamic-update-slice(f32[4,512,2,128]{1,0,3,2:T(4,128)} %get-tuple-element.758, f32[1,512,2,128]{1,0,3,2:T(1,128)S(1)} %copy.278, s32[]{:T(128)S(6)} %copy.291, s32[]{:T(128)} %constant.105.clone.1..sunk.1, s32[]{:T(128)} %constant.105.clone.1..sunk.1, s32[]{:T(128)} %constant.105.clone.1..sunk.1) | dynamic-update-slice | bytes 1048580 | tf_op jit(solution)/shard_map/while/body/jit(dynamic_update_index_in_dim)/dynamic_update_slice | solution.py:190
  81.0 11.1 %dynamic_update_slice.12 = f32[4,512,2,128]{1,0,3,2:T(4,128)} dynamic-update-slice(f32[4,512,2,128]{1,0,3,2:T(4,128)} %get-tuple-element.758, f32[1,512,2,128]{1,0,3,2:T(1,128)S(1)} %copy.278, s32[]{:T(128)S(6)} %copy.291, s32[]{:T(128)} %constant.105.clone.1..sunk.1, s32[]{:T(128)} %constant.105.clone.1..sunk.1, s32[]{:T(128)} %constant.105.clone.1..sunk.1) | dynamic-update-slice | bytes 1048580 | tf_op jit(solution)/shard_map/while/body/jit(dynamic_update_index_in_dim)/dynamic_update_slice | solution.py:190
  106.0 11.1 %dynamic_update_slice.12 = f32[4,512,2,128]{1,0,3,2:T(4,128)} dynamic-update-slice(f32[4,512,2,128]{1,0,3,2:T(4,128)} %get-tuple-element.758, f32[1,512,2,128]{1,0,3,2:T(1,128)S(1)} %copy.278, s32[]{:T(128)S(6)} %copy.291, s32[]{:T(128)} %constant.105.clone.1..sunk.1, s32[]{:T(128)} %constant.105.clone.1..sunk.1, s32[]{:T(128)} %constant.105.clone.1..sunk.1) | dynamic-update-slice | bytes 1048580 | tf_op jit(solution)/shard_map/while/body/jit(dynamic_update_index_in_dim)/dynamic_update_slice | solution.py:190
  131.0 11.1 %dynamic_update_slice.12 = f32[4,512,2,128]{1,0,3,2:T(4,128)} dynamic-update-slice(f32[4,512,2,128]{1,0,3,2:T(4,128)} %get-tuple-element.758, f32[1,512,2,128]{1,0,3,2:T(1,128)S(1)} %copy.278, s32[]{:T(128)S(6)} %copy.291, s32[]{:T(128)} %constant.105.clone.1..sunk.1, s32[]{:T(128)} %constant.105.clone.1..sunk.1, s32[]{:T(128)} %constant.105.clone.1..sunk.1) | dynamic-update-slice | bytes 1048580 | tf_op jit(solution)/shard_map/while/body/jit(dynamic_update_index_in_dim)/dynamic_update_slice | solution.py:190
  176.7 64.1 %while.41 = (s32[]{:T(128)}, f32[2,1024,2,128]{1,0,3,2:T(2,128)}, bf16[2,1024,2,128]{3,1,2,0:T(8,128)(2,1)}, bf16[16,2,128]{2,0,1:T(8,128)(2,1)S(1)}, s32[2,1024...) while((s32[]{:T(128)}, f32[2,1024,2,128]{1,0,3,2:T(2,128)}, ...), condition=%wide.region_6.7_spmd, body=%wide.region_1.6_spmd.sunk | while | flops 1119318016 | bytes 39351420 | solution.py:231
  189.9 18.8 %dynamic_update_slice.11 = f32[2,1024,2,128]{1,0,3,2:T(2,128)} dynamic-update-slice(f32[2,1024,2,128]{1,0,3,2:T(2,128)} %get-tuple-element.723, f32[1,1024,2,128]{1,0,3,2:T(1,128)S(1)} %copy.275, s32[]{:T(128)S(6)} %copy.283, s32[]{:T(128)} %constant.105.clone.1..sunk, s32[]{:T(128)} %constant.105.clone.1..sunk, s32[]{:T(128)} %constant.105.clone.1..sunk) | dynamic-update-slice | bytes 2097156 | tf_op jit(solution)/shard_map/while/body/jit(dynamic_update_index_in_dim)/dynamic_update_slice | solution.py:231
  221.9 18.8 %dynamic_update_slice.11 = f32[2,1024,2,128]{1,0,3,2:T(2,128)} dynamic-update-slice(f32[2,1024,2,128]{1,0,3,2:T(2,128)} %get-tuple-element.723, f32[1,1024,2,128]{1,0,3,2:T(1,128)S(1)} %copy.275, s32[]{:T(128)S(6)} %copy.283, s32[]{:T(128)} %constant.105.clone.1..sunk, s32[]{:T(128)} %constant.105.clone.1..sunk, s32[]{:T(128)} %constant.105.clone.1..sunk) | dynamic-update-slice | bytes 2097156 | tf_op jit(solution)/shard_map/while/body/jit(dynamic_update_index_in_dim)/dynamic_update_slice | solution.py:231
  247.0 25.8 %all-gather.2 = f32[32,1,2]{2,1,0:T(1,128)} all-gather(f32[1,1,2]{2,1,0:T(1,128)S(1)} %bitcast.267), channel_id=1, replica_groups=mesh['req'=32,'tp'=4] {'req'}, dimensions={0}, use_global_device_ids=true | all-gather | bytes 264 | tf_op jit(solution)/shard_map/all_gather | solution.py:18
  277.9 62.8 %all-reduce.2 = (f32[32]{0:T(128)}, f32[32]{0:T(128)}) all-reduce(f32[32]{0:T(128)} %convert_dynamic-update-slice_fusion.1, f32[32]{0:T(128)} %convert_dynamic-update-slice_fusion), channel_id=1, replica_groups=mesh['req'=32,'tp'=4] {'req'}, use_global_device_ids=true, to_apply=%add | all-reduce | flops 64 | bytes 512
  340.8 238.4 %while.43 = (s32[]{:T(128)}, f32[2,128,128]{2,1,0:T(8,128)}, f32[]{:T(128)}, s32[]{:T(128)}, f32[32,2]{1,0:T(8,128)}, /*index=5*/f32[32]{0:T(128)}, f32[32,2,128...) while((s32[]{:T(128)}, f32[2,128,128]{2,1,0:T(8,128)}, ...), condition=%wide.region_16.17_spmd.clone, body=%wide.region_15.16_spmd.clone.sunk | while | flops 131087 | bytes 393486 | solution.py:30
  591.3 158.3 %all-reduce.5.cloned.1.call-done = f32[2048,1024]{1,0:T(8,128)} async-done(((f32[2048,1024]{1,0:T(8,128)}), f32[2048,1024]{1,0:T(8,128)}) %all-reduce.5.cloned.1.call-update) | async-done | bytes 8388624 | tf_op jit(solution)/shard_map/psum | solution.py:241
  762.6 11.2 %convolution_convert_fusion.2 = bf16[2048,1024]{1,0:T(8,128)(2,1)} fusion(bf16[704,1024]{1,0:T(8,128)(2,1)S(1)} %copy-done, f32[2048,704]{0,1:T(8,128)} %fusion.78, bf16[1024,704]{0,1:T(8,128)(2,1)} %param.35, bf16[2048,1024]{1,0:T(8,128)(2,1)} %copy-done.1, f32[1024]{0:T(1024)S(1)} %convert_element_type.187, f32[2048]{0:T(1024)S(1)} %add_rsqrt_fusion.3), kind=kOutput, calls=%fused_computation.108 | convolution fusion | flops 5924716544 | bytes 17051648 | tf_op jit(solution)/shard_map/dot_general | solution.py:249
  775.9 8.2 all-to-all-start
  791.7 5.9 pad_maximum_fusion
  805.5 6.9 reduce.11
  812.4 6.6 reshape.366
  819.0 7.8 all-to-all-start.1
  827.1 51.7 %all-to-all-done.1 = bf16[32,2,32768]{2,1,0:T(2,128)(2,1)} async-done(((bf16[32,2,32768]{2,1,0:T(2,128)(2,1)}), bf16[32,2,32768]{2,1,0:T(2,128)(2,1)}, u32[]{:S(2)}, u32[]{:S(2)}) %all-to-all-start.1) | async-done | bytes 4194336 | tf_op jit(solution)/shard_map/all_to_all | solution.py:137
  878.8 19.8 %reshape.367 = bf16[32,1,65536]{2,1,0:T(2,128)(2,1)} reshape(bf16[32,2,32768]{2,1,0:T(2,128)(2,1)} %all-to-all-done.1) | data formatting | bytes 8388608
  898.6 7.9 convolution_convert_fusion.1
  908.6 19.3 %all-gather.8.cloned.1.call-done = bf16[8192,1024]{1,0:T(8,128)(2,1)} async-done(((bf16[2048,1024]{1,0:T(8,128)(2,1)}), bf16[8192,1024]{1,0:T(8,128)(2,1)}) %all-gather.8.cloned.1.call-update) | async-done | bytes 16777232 | tf_op jit(solution)/shard_map/all_gather | solution.py:248
  927.9 12.0 %reduce_sum.98 = bf16[2048,1024]{1,0:T(8,128)(2,1)} reduce(bf16[4,2048,1024]{2,1,0:T(8,128)(2,1)} %bitcast.245, bf16[]{:T(256)} %constant.117.clone.1), dimensions={0}, to_apply=%region_20.21 | reduce | flops 6291456 | bytes 20971522 | tf_op jit(solution)/shard_map/reduce_sum | solution.py:247
  939.9 7.6 fusion.69
  (353 shorter events, 358.8 us)
Async XLA Ops:
  7.2 755.4 %copy-start = (bf16[704,1024]{1,0:T(8,128)(2,1)S(1)}, bf16[704,1024]{1,0:T(8,128)(2,1)}, u32[]{:S(2)}) copy-start(bf16[704,1024]{1,0:T(8,128)(2,1)} %param.36) | copy-start | bytes 4325380
  7.2 4.0 copy-start.15
  7.2 333.6 %all-gather.6.cloned.1.call-start = ((), (), s32[]{:S(2)}) async-start(), calls=%async_computation.3 | async-start | bytes 4325376 | tf_op jit(solution)/shard_map/all_gather | solution.py:18
  14.9 1.6 copy-start.6
  19.2 4.1 copy-start.2
  19.2 4.1 copy-start.22
  23.2 123.7 %copy-start.4 = (bf16[2048,256]{0,1:T(8,128)(2,1)}, bf16[2048,256]{0,1:T(8,128)(2,1)S(1)}, u32[]{:S(2)}) copy-start(bf16[2048,256]{0,1:T(8,128)(2,1)S(1)} %get-tuple-element.534) | copy-start | bytes 3145732
  26.0 12.3 %copy-start.11 = (f32[2048,2]{0,1:T(2,128)}, f32[2048,2]{0,1:T(2,128)S(1)}, u32[]{:S(2)}) copy-start(f32[2048,2]{0,1:T(2,128)S(1)} %add_rsqrt_fusion.1) | copy-start | bytes 49156
  38.3 4.2 copy-start.14
  143.4 606.1 %all-reduce.5.cloned.1.call-start = ((), (), s32[]{:S(2)}) async-start(), calls=%async_computation.2 | async-start | bytes 16777216 | tf_op jit(solution)/shard_map/psum | solution.py:241
  172.9 3.7 copy-start.16
  172.9 3.7 copy-start.17
  240.7 340.0 %copy-start.8 = (f32[2048,2,128]{2,0,1:T(8,128)S(1)}, f32[2048,2,128]{2,0,1:T(8,128)}, u32[]{:S(2)}) copy-start(f32[2048,2,128]{2,0,1:T(8,128)} %copy.220) | copy-start | bytes 6291460
  240.7 340.0 %copy-start.12 = (f32[2048,2]{0,1:T(2,128)S(1)}, f32[2048,2]{0,1:T(2,128)}, u32[]{:S(2)}) copy-start(f32[2048,2]{0,1:T(2,128)} %copy-done.11) | copy-start | bytes 49156
  579.2 6.0 copy-start.9
  579.2 6.0 copy-start.19
  585.1 1.0 copy-start.10
  590.6 337.3 %all-gather.8.cloned.1.call-start = ((), (), s32[]{:S(2)}) async-start(), calls=%async_computation.4 | async-start | bytes 20971520 | tf_op jit(solution)/shard_map/all_gather | solution.py:248
  591.3 166.1 %copy-start.21 = (bf16[1024,704]{0,1:T(8,128)(2,1)S(1)}, bf16[1024,704]{0,1:T(8,128)(2,1)}, u32[]{:S(2)}) copy-start(bf16[1024,704]{0,1:T(8,128)(2,1)} %param.34) | copy-start | bytes 4325380
  755.4 2.0 copy-start.1
  773.8 10.4 %copy-start.5 = (bf16[2048,256]{0,1:T(8,128)(2,1)S(1)}, bf16[2048,256]{0,1:T(8,128)(2,1)}, u32[]{:S(2)}) copy-start(bf16[2048,256]{0,1:T(8,128)(2,1)} %copy-done.4) | copy-start | bytes 3145732
  773.8 14.1 %copy-start.7 = (bf16[2048,256]{0,1:T(8,128)(2,1)S(1)}, bf16[2048,256]{0,1:T(8,128)(2,1)}, u32[]{:S(2)}) copy-start(bf16[2048,256]{0,1:T(8,128)(2,1)} %copy-done.6) | copy-start | bytes 3145732
  775.9 43.1 %all-to-all-start = ((bf16[32,1,1]{2,1,0:T(2,128)(2,1)}), bf16[32,1,1]{2,1,0:T(2,128)(2,1)S(1)}, u32[]{:S(2)}, u32[]{:S(2)}) async-start(bf16[32,1,1]{2,1,0:T(2,128)(2,1)} %copy.222), calls=%async_computation | async-start | bytes 32768 | tf_op jit(solution)/shard_map/all_to_all | solution.py:138
  819.0 59.8 %all-to-all-start.1 = ((bf16[32,2,32768]{2,1,0:T(2,128)(2,1)}), bf16[32,2,32768]{2,1,0:T(2,128)(2,1)}, u32[]{:S(2)}, u32[]{:S(2)}) async-start(bf16[32,2,32768]{2,1,0:T(2,128)(2,1)} %reshape.366), calls=%async_computation.1 | async-start | bytes 8388608 | tf_op jit(solution)/shard_map/all_to_all | solution.py:137
  (6 other events, 3.9 us)
Sparse Core Ops, SparseCore 0:
  143.6 50.0 all-gather.5
  590.8 158.7 all-reduce.4
  773.9 153.9 all-gather.7
